TPU v7x, 32 devices: a whole 2x2x4 slice. The times are simulated.
32 devices in a mesh: groups: 2 (over x), seq: 8 (over z, y), chan: 2 (over core).
Axes of the slice: x: 2, y: 2, z: 4, core: 2. Of those that a mesh axis runs over, the one named last changes fastest.
Arguments:
- inputs: bfloat16 [8192, 768], P(('groups', 'seq')), parts along dimension 0, may hold values from -6 to 6
- enc_weight: bfloat16 [768, 5, 1536], P('seq', None, 'chan'), may hold values from -0.09375 to 0.09375
- dec_weight: bfloat16 [768, 5, 1536], P('seq', None, 'chan'), may hold values from -0.0625 to 0.0625
- cotangent: bfloat16 [8192, 768], P(('groups', 'seq'), 'chan'), parts along dimension 0, may hold values from -6 to 6
Outputs:
- mixed_out: bfloat16 [8192, 768], P(('groups', 'seq'), 'chan'), parts along dimension 0
- input_grad: bfloat16 [8192, 768], P(('groups', 'seq'), 'chan'), parts along dimension 0
- enc_grad: bfloat16 [1536, 5, 1536], P(('groups', 'seq'), None, 'chan'), parts along dimension 0
- dec_grad: bfloat16 [1536, 5, 1536], P(('groups', 'seq'), None, 'chan'), parts along dimension 0
There are 2 independent parts, one for each index of `groups`. A program takes and returns all parts, laid end to end along the dimension named above; an argument that names none is the same for every part. Nothing has to cross between parts.
All inputs are finite; a program needn't handle non-finite values.
Results may differ from a plain program's by a relative error of at most 0.012.
Values may be sent and summed in bfloat16 or wider, within the bound.
A program may use at most 128 MiB of HBM per device.

v0:
```python
import jax
import jax.numpy as jnp
from jax import lax
from jax.sharding import PartitionSpec as P


def with_halo(array, sides, width):
    for axis, dim in sides:
        size, length = (lax.axis_size(axis), array.shape[dim])
        up = [(i, (i + 1) % size) for i in range(size - 1)]
        down = [(j, i) for i, j in up]
        last = lax.slice_in_dim(array, length - width, length, axis=dim)
        first = lax.slice_in_dim(array, 0, width, axis=dim)
        before = lax.ppermute(last, axis, up)
        after = lax.ppermute(first, axis, down)
        array = jnp.concatenate([before, array, after], axis=dim)
    return array


def gelu_fn(values):
    return jax.nn.gelu(values, approximate=True)


def shards(inputs, enc_weight, dec_weight, cotangent):
    row_count = inputs.shape[0]
    half_rows = row_count // 2
    fine_width = inputs.shape[1]
    share_width = cotangent.shape[1]
    taps = enc_weight.shape[1]
    coarse_share = enc_weight.shape[2]
    contract_last = (((1,), (1,)), ((), ()))
    enc_full = lax.all_gather(enc_weight, "seq", axis=0, tiled=True)
    dec_full = lax.all_gather(dec_weight, "seq", axis=0, tiled=True)
    pooled = (
        inputs.astype(jnp.float32).reshape(half_rows, 2, fine_width).sum(axis=1) * 0.5
    ).astype(jnp.bfloat16)
    pad_pool = with_halo(pooled, (("seq", 0),), 2)
    pre_act = jnp.zeros((half_rows, coarse_share), jnp.float32)
    for tap_index in range(taps):
        pre_act = pre_act + jnp.dot(
            pad_pool[tap_index : tap_index + half_rows],
            enc_full[:, tap_index, :],
            preferred_element_type=jnp.float32,
        )
    hidden = gelu_fn(pre_act).astype(jnp.bfloat16)
    pad_hidden = with_halo(hidden, (("seq", 0),), 1)
    pad_up = jnp.repeat(pad_hidden, 2, axis=0)
    dec_part = jnp.zeros((row_count, fine_width), jnp.float32)
    for tap_index in range(taps):
        dec_part = dec_part + lax.dot_general(
            pad_up[tap_index : tap_index + row_count],
            dec_full[:, tap_index, :],
            contract_last,
            preferred_element_type=jnp.float32,
        )
    dec_share = lax.psum_scatter(
        dec_part.astype(jnp.bfloat16), "chan", scatter_dimension=1, tiled=True
    ).astype(jnp.float32)
    col_start = lax.axis_index("chan") * share_width
    skip_cols = lax.dynamic_slice_in_dim(inputs, col_start, share_width, 1)
    mixed_out = (skip_cols.astype(jnp.float32) + dec_share).astype(jnp.bfloat16)
    cot_full = lax.all_gather(cotangent, "chan", axis=1, tiled=True)
    pad_cot = with_halo(cot_full, (("seq", 0),), 2)
    up_grad = jnp.zeros((row_count, coarse_share), jnp.float32)
    for tap_index in range(taps):
        up_grad = up_grad + jnp.dot(
            pad_cot[4 - tap_index : 4 - tap_index + row_count],
            dec_full[:, tap_index, :],
            preferred_element_type=jnp.float32,
        )
    hid_grad = up_grad.reshape(half_rows, 2, coarse_share).sum(axis=1)
    _, pullback = jax.vjp(gelu_fn, pre_act)
    pre_grad = pullback(hid_grad)[0].astype(jnp.bfloat16)
    pad_grad = with_halo(pre_grad, (("seq", 0),), 2)
    pool_grad = jnp.zeros((half_rows, fine_width), jnp.float32)
    for tap_index in range(taps):
        pool_grad = pool_grad + lax.dot_general(
            pad_grad[4 - tap_index : 4 - tap_index + half_rows],
            enc_full[:, tap_index, :],
            contract_last,
            preferred_element_type=jnp.float32,
        )
    total_sum = lax.psum(pool_grad.astype(jnp.bfloat16), "chan").astype(jnp.float32)
    grad_share = lax.dynamic_slice_in_dim(total_sum, col_start, share_width, 1)
    input_grad = (cotangent.astype(jnp.float32) + 0.5 * jnp.repeat(grad_share, 2, axis=0)).astype(
        jnp.bfloat16
    )

    def dec_terms():
        return jnp.stack(
            [
                jnp.dot(
                    cot_full.T,
                    pad_up[tap_index : tap_index + row_count],
                    preferred_element_type=jnp.float32,
                )
                for tap_index in range(taps)
            ],
            axis=1,
        )

    joint_sum = lax.psum_scatter(
        jnp.concatenate(
            [
                jnp.stack(
                    [
                        jnp.dot(
                            pad_pool[tap_index : tap_index + half_rows].T,
                            pre_grad,
                            preferred_element_type=jnp.float32,
                        )
                        for tap_index in range(taps)
                    ],
                    axis=1,
                ),
                dec_terms(),
            ],
            axis=2,
        ).astype(jnp.bfloat16),
        "seq",
        scatter_dimension=0,
        tiled=True,
    ).astype(jnp.float32)
    enc_sum = joint_sum[:, :, :coarse_share]
    dec_sum = joint_sum[:, :, coarse_share:]
    return (mixed_out, input_grad, enc_sum.astype(jnp.bfloat16), dec_sum.astype(jnp.bfloat16))


def solution(mesh):
    return jax.shard_map(
        shards,
        mesh=mesh,
        in_specs=(
            P(("groups", "seq"), None),
            P("seq", None, "chan"),
            P("seq", None, "chan"),
            P(("groups", "seq"), "chan"),
        ),
        out_specs=(
            P(("groups", "seq"), "chan"),
            P(("groups", "seq"), "chan"),
            P(("groups", "seq"), None, "chan"),
            P(("groups", "seq"), None, "chan"),
        ),
        check_vma=False,
    )
```

profile of v0, /device:TPU:0, one launch (start us, length us, event | category | flops | bytes accessed | tf_op | source)
XLA Modules:
  0.0 509.0 jit_solution(5221697619440300852)
XLA Ops:
  8.7 2.7 all_gather.11
  11.4 1.3 collective-permute-start.4
  12.7 5.4 %collective-permute-start.5 = (bf16[2,768]{1,0:T(2,128)(2,1)S(1)}, bf16[2,768]{1,0:T(2,128)(2,1)S(1)}, u32[]{:S(2)}, u32[]{:S(2)}) collective-permute-start(bf16[2,768]{1,0:T(2,128)(2,1)S(1)} %get-tuple-element.17), channel_id=1, source_target_pairs={{0,2},{2,4},{4,6},{6,8},{8,10},{10,12},{12,14},{1,3},{3,5},{5,7},{... | collective-permute-start | bytes 9224 | tf_op jit(solution)/shard_map/ppermute | solution.py:14
  18.9 1.9 reduce_sum.18
  20.8 4.8 collective-permute-start
  25.7 1.5 collective-permute-start.1
  27.2 80.0 %all-gather.5.cloned.1.call-done = bf16[768,5,768]{2,0,1:T(8,128)(2,1)} async-done(((bf16[96,5,768]{2,0,1:T(8,128)(2,1)}), bf16[768,5,768]{2,0,1:T(8,128)(2,1)}) %all-gather.5.cloned.1.call-update) | async-done | bytes 5898256 | tf_op jit(solution)/shard_map/all_gather | solution.py:33
  107.2 2.2 fusion.37
  109.4 2.1 fusion.33
  113.1 2.1 add_add_fusion
  115.2 86.7 %all-gather.3.cloned.1.call-done = bf16[768,5,768]{2,0,1:T(8,128)(2,1)} async-done(((bf16[96,5,768]{2,0,1:T(8,128)(2,1)}), bf16[768,5,768]{2,0,1:T(8,128)(2,1)}) %all-gather.3.cloned.1.call-update) | async-done | bytes 5898256 | tf_op jit(solution)/shard_map/all_gather | solution.py:32
  201.9 1.7 fusion.28
  203.6 2.6 fusion.30
  206.3 2.2 reshape.29
  208.5 2.9 reduce_sum.19
  211.4 1.8 fusion.26
  213.2 1.9 fusion.23
  215.1 2.2 fusion.48
  218.5 1.3 collective-permute-start.6
  219.8 4.5 collective-permute-start.7
  224.4 3.4 collective-permute-start.2
  227.7 1.5 collective-permute-start.3
  231.5 2.7 fusion.27
  234.2 3.2 fusion.36
  238.5 2.5 copy-done
  241.5 1.2 reshape.28
  244.0 1.2 slice.169
  245.2 2.4 fusion.38
  247.7 2.2 fusion.34
  249.9 2.2 fusion.32
  252.2 2.3 add_convert_fusion
  254.5 1.9 fusion.1
  256.9 1.3 fusion.25
  258.2 1.2 fusion.21
  259.4 1.3 fusion.24
  261.1 3.1 fusion.3
  264.1 1.2 copy.12
  265.3 1.9 fusion.5
  267.3 1.8 fusion.7
  269.1 1.9 fusion.9
  271.0 10.2 %pad_maximum_fusion = bf16[768,5,1536]{0,2,1:T(8,128)(2,1)} fusion(bf16[768,5,768]{0,2,1:T(8,128)(2,1)} %fusion.9, bf16[768,5,768]{0,2,1:T(8,128)(2,1)} %copy-done), kind=kLoop, calls=%fused_computation | loop fusion | flops 23592960 | bytes 23592960 | tf_op jit(solution)/shard_map/concatenate | solution.py:103
  281.2 16.4 %copy.16 = bf16[768,7680]{1,0:T(8,128)(2,1)} copy(bf16[768,7680]{0,1:T(8,128)(2,1)} %bitcast.119) | data formatting | bytes 23592960
  300.4 1.2 copy.13
  302.5 192.3 %reduce-scatter.9.cloned.1.call-done = bf16[96,7680]{1,0:T(8,128)(2,1)} async-done(((bf16[768,7680]{1,0:T(8,128)(2,1)}), bf16[96,7680]{1,0:T(8,128)(2,1)}) %reduce-scatter.9.cloned.1.call-update) | async-done | bytes 1474576
  494.8 2.7 copy.17
  497.5 1.5 fusion.78
  499.0 2.3 copy.11
  501.2 1.2 copy.10
  (87 shorter events, 14.7 us)
Async XLA Ops:
  7.2 10.9 %copy-start.3 = (bf16[512,768]{1,0:T(8,128)(2,1)S(1)}, bf16[512,768]{1,0:T(8,128)(2,1)}, u32[]{:S(2)}) copy-start(bf16[512,768]{1,0:T(8,128)(2,1)} %param.4) | copy-start | bytes 2359300
  7.2 100.0 %all-gather.5.cloned.1.call-start = ((), (), s32[]{:S(2)}) async-start(), calls=%async_computation.3 | async-start | bytes 6635520 | tf_op jit(solution)/shard_map/all_gather | solution.py:33
  7.9 194.0 %all-gather.3.cloned.1.call-start = ((), (), s32[]{:S(2)}) async-start(), calls=%async_computation.2 | async-start | bytes 6635520 | tf_op jit(solution)/shard_map/all_gather | solution.py:32
  8.7 289.0 %all-reduce.2.cloned.1.call-start = ((), (), s32[]{:S(2)}) async-start(), calls=%async_computation.4 | async-start | bytes 786432 | tf_op jit(solution)/shard_map/psum | solution.py:83
  11.4 15.8 %collective-permute-start.4 = (bf16[2,768]{1,0:T(2,128)(2,1)S(1)}, bf16[2,768]{1,0:T(2,128)(2,1)S(1)}, u32[]{:S(2)}, u32[]{:S(2)}) collective-permute-start(bf16[2,768]{1,0:T(2,128)(2,1)S(1)} %get-tuple-element.16), channel_id=1, source_target_pairs={{2,0},{4,2},{6,4},{8,6},{10,8},{12,10},{14,12},{3,1},{5,3},{7,5},{... | collective-permute-start | bytes 9224 | tf_op jit(solution)/shard_map/ppermute | solution.py:15
  12.7 14.6 %collective-permute-start.5 = (bf16[2,768]{1,0:T(2,128)(2,1)S(1)}, bf16[2,768]{1,0:T(2,128)(2,1)S(1)}, u32[]{:S(2)}, u32[]{:S(2)}) collective-permute-start(bf16[2,768]{1,0:T(2,128)(2,1)S(1)} %get-tuple-element.17), channel_id=1, source_target_pairs={{0,2},{2,4},{4,6},{6,8},{8,10},{10,12},{12,14},{1,3},{3,5},{5,7},{... | collective-permute-start | bytes 9224 | tf_op jit(solution)/shard_map/ppermute | solution.py:14
  20.8 190.6 %collective-permute-start = (bf16[2,768]{1,0:T(2,128)(2,1)S(1)}, bf16[2,768]{1,0:T(2,128)(2,1)S(1)}, u32[]{:S(2)}, u32[]{:S(2)}) collective-permute-start(bf16[2,768]{1,0:T(2,128)(2,1)S(1)} %get-tuple-element.24), channel_id=1, source_target_pairs={{0,2},{2,4},{4,6},{6,8},{8,10},{10,12},{12,14},{1,3},{3,5},{5,7},{... | collective-permute-start | bytes 9224 | tf_op jit(solution)/shard_map/ppermute | solution.py:14
  25.7 178.0 %collective-permute-start.1 = (bf16[2,768]{1,0:T(2,128)(2,1)S(1)}, bf16[2,768]{1,0:T(2,128)(2,1)S(1)}, u32[]{:S(2)}, u32[]{:S(2)}) collective-permute-start(bf16[2,768]{1,0:T(2,128)(2,1)S(1)} %get-tuple-element.25), channel_id=1, source_target_pairs={{2,0},{4,2},{6,4},{8,6},{10,8},{12,10},{14,12},{3,1},{5,3},{7,5},{... | collective-permute-start | bytes 9224 | tf_op jit(solution)/shard_map/ppermute | solution.py:15
  107.2 4.3 copy-start.7
  203.6 11.5 %copy-start.14 = (bf16[2,768]{1,0:T(2,128)(2,1)}, bf16[2,768]{1,0:T(2,128)(2,1)S(1)}, u32[]{:S(2)}) copy-start(bf16[2,768]{1,0:T(2,128)(2,1)S(1)} %collective-permute-done.1) | copy-start | bytes 9220
  213.2 1.9 copy-start.10
  213.2 1.9 copy-start.16
  218.5 38.4 %collective-permute-start.6 = (bf16[2,768]{1,0:T(2,128)(2,1)}, bf16[2,768]{1,0:T(2,128)(2,1)}, u32[]{:S(2)}, u32[]{:S(2)}) collective-permute-start(bf16[2,768]{1,0:T(2,128)(2,1)} %get-tuple-element.18), channel_id=1, source_target_pairs={{2,0},{4,2},{6,4},{8,6},{10,8},{12,10},{14,12},{3,1},{5,3},{7,5},{... | collective-permute-start | bytes 9224 | tf_op jit(solution)/shard_map/ppermute | solution.py:15
  219.8 36.6 %collective-permute-start.7 = (bf16[2,768]{1,0:T(2,128)(2,1)}, bf16[2,768]{1,0:T(2,128)(2,1)S(1)}, u32[]{:S(2)}, u32[]{:S(2)}) collective-permute-start(bf16[2,768]{1,0:T(2,128)(2,1)} %get-tuple-element.19), channel_id=1, source_target_pairs={{0,2},{2,4},{4,6},{6,8},{8,10},{10,12},{12,14},{1,3},{3,5},{5,7},{... | collective-permute-start | bytes 9224 | tf_op jit(solution)/shard_map/ppermute | solution.py:14
  224.4 16.6 %collective-permute-start.2 = (bf16[1,768]{1,0:T(2,128)(2,1)}, bf16[1,768]{1,0:T(2,128)(2,1)S(1)}, u32[]{:S(2)}, u32[]{:S(2)}) collective-permute-start(bf16[1,768]{1,0:T(2,128)(2,1)} %get-tuple-element.22), channel_id=1, source_target_pairs={{0,2},{2,4},{4,6},{6,8},{8,10},{10,12},{12,14},{1,3},{3,5},{5,7},{... | collective-permute-start | bytes 4616 | tf_op jit(solution)/shard_map/ppermute | solution.py:14
  227.7 13.3 %collective-permute-start.3 = (bf16[1,768]{1,0:T(2,128)(2,1)}, bf16[1,768]{1,0:T(2,128)(2,1)S(1)}, u32[]{:S(2)}, u32[]{:S(2)}) collective-permute-start(bf16[1,768]{1,0:T(2,128)(2,1)} %get-tuple-element.23), channel_id=1, source_target_pairs={{2,0},{4,2},{6,4},{8,6},{10,8},{12,10},{14,12},{3,1},{5,3},{7,5},{... | collective-permute-start | bytes 4616 | tf_op jit(solution)/shard_map/ppermute | solution.py:15
  230.0 4.2 copy-start.11
  234.2 3.2 copy-start.15
  238.5 2.5 copy-start
  245.2 2.4 copy-start.8
  247.7 2.3 copy-start.13
  247.7 4.5 copy-start.6
  249.9 6.4 %slice-start = ((s8[5898240]{0:T(1024)(128)(4,1)}), s8[4194304]{0:T(1024)(128)(4,1)S(1)}, s32[]{:S(2)}) async-start(s8[5898240]{0:T(1024)(128)(4,1)} %bitcast.121), calls=%async_computation.7 | async-start | bytes 8388608
  252.2 4.2 slice-start.1
  256.9 1.3 copy-start.2
  260.8 4.6 copy-start.12
  260.8 39.6 %reduce-scatter.7.cloned.1.call-start = ((), (), s32[]{:S(2)}) async-start(), calls=%async_computation.5 | async-start | bytes 1179648
  265.3 1.9 copy-start.9
  267.2 227.6 %reduce-scatter.9.cloned.1.call-start = ((), (), s32[]{:S(2)}) async-start(), calls=%async_computation.6 | async-start | bytes 13271040
  297.7 1.9 copy-start.5
  299.0 2.6 copy-start.4
  499.0 2.3 copy-start.1
Sparse Core Ops, SparseCore 0:
  10.2 96.9 all-gather.4
  109.4 92.4 all-gather.2
  260.9 19.2 all-reduce.1
  282.3 9.3 reduce-scatter.6
  297.8 196.9 reduce-scatter.8
where the time goes:
time: 510 us; the launch traced here: 509 us
  waiting for transfers between devices  360 us (71%)
  matrix products  50.6 us (10%)
  local copies, waits for them, and re-layouts  38.8 us (8%)
  starting transfers between devices  24.2 us (5%)
  other arithmetic  18 us (4%)
  between operations  14.4 us (3%)
    unnamed x7, waiting for transfers between devices  194 us
    all_gather x1, waiting for transfers between devices, shards(): enc_full = lax.all_gather(enc_weight, 'seq', axis=0, tiled=True)  86.7 us
    all_gather x1, waiting for transfers between devices, shards(): dec_full = lax.all_gather(dec_weight, 'seq', axis=0, tiled=True)  80 us
    unnamed x45, local copies, waits for them, and re-layouts  27.7 us
    ppermute x4, starting transfers between devices, with_halo(): before = lax.ppermute(last, axis, up)  18.1 us
    dot_general x5, matrix products, shards(): lax.dot_general(pad_up[tap_index:tap_index + row_count], dec_full[:, tap_...  12.4 us
    dot_general x5, matrix products, dec_terms(): jnp.dot(cot_full.T, pad_up[tap_index:tap_index + row_count], preferred_el...  10.5 us
    dot_general x5, matrix products, shards(): jnp.dot(pad_pool[tap_index:tap_index + half_rows], enc_full[:, tap_index,...  10.2 us
  transfers between devices with their start and end apart: 13, of which 3 were waited for; matrix products, arithmetic and copies ran while one was open for 17% of the time, Pallas kernels for 0%

commit v1 on v0

--- a/solution.py
+++ b/solution.py
@@ -1,7 +1,27 @@
+import functools
 import jax
 import jax.numpy as jnp
 from jax import lax
 from jax.sharding import PartitionSpec as P
+
+
+def search_rails_for(obj, axis_id):
+    a_next = lax.psum(1, axis_id)
+    even = lax.axis_index(axis_id)
+    w_next, z, outer = (a_next, even, obj.shape[0])
+    inbox = tuple((t * w_next if p == 0 else t for p, t in enumerate(obj.shape)))
+    u_next = jnp.zeros(inbox, obj.dtype)
+    y2 = lax.dynamic_update_slice_in_dim(u_next, obj, z * outer, axis=0)
+    tick = 1
+    while tick < w_next:
+        oldest = tuple(((p, (p + 1) % w_next) for p in range(w_next)))
+        obj = lax.ppermute(obj, axis_id, oldest)
+        y2 = lax.dynamic_update_slice_in_dim(y2, obj, (z - tick) % w_next * outer, axis=0)
+        tick += 1
+    return y2
+
+
+compute_regions_over_axis = functools.partial(search_rails_for, axis_id="seq")
 
 
 def with_halo(array, sides, width):
@@ -30,7 +50,7 @@
     coarse_share = enc_weight.shape[2]
     contract_last = (((1,), (1,)), ((), ()))
     enc_full = lax.all_gather(enc_weight, "seq", axis=0, tiled=True)
-    dec_full = lax.all_gather(dec_weight, "seq", axis=0, tiled=True)
+    dec_full = compute_regions_over_axis(dec_weight)
     pooled = (
         inputs.astype(jnp.float32).reshape(half_rows, 2, fine_width).sum(axis=1) * 0.5
     ).astype(jnp.bfloat16)

time: 510 us -> 537 us (1.053)
  matrix products: 50.6 us -> 66.3 us
  local copies, waits for them, and re-layouts: 38.8 us -> 53.5 us
    ppermute x0 -> x7, waiting for transfers between devices: none -> 164 us  [search_rails_for(): obj = lax.ppermute(obj, axis_id, oldest)]
    all_gather x1, waiting for transfers between devices: 86.7 us -> 0.02 us  [shards(): enc_full = lax.all_gather(enc_weight, 'seq', axis=0, tiled=True)]
    all_gather x1 -> x0, waiting for transfers between devices: 80 us -> none  [shards(): dec_full = lax.all_gather(dec_weight, 'seq', axis=0, tiled=True)]
    dynamic_update_slice x0 -> x8, local copies, waits for them, and re-layouts: none -> 12 us  [the longest x7 11 us: search_rails_for(): lax.dynamic_update_slice_in_dim(y2, obj, (z - tick) % w_next * outer, axi...]
    ppermute x4, starting transfers between devices: 18.1 us -> 12.3 us  [with_halo(): before = lax.ppermute(last, axis, up)]
    dot_general x5, matrix products: 12.4 us -> 18.1 us  [shards(): lax.dot_general(pad_up[tap_index:tap_index + row_count], dec_full[:, tap_...]
    unnamed x7 -> x6, waiting for transfers between devices: 194 us -> 196 us
    unnamed x45 -> x33, local copies, waits for them, and re-layouts: 27.7 us -> 26.2 us
  transfers between devices with their start and end apart: 13 -> 19, of which waited for: 3 -> 8; matrix products, arithmetic and copies ran while one was open for 17% -> 21% of each run, Pallas kernels for 0% -> 0%
where the time goes in v1:
time: 537 us; the launch traced here: 535 us
  waiting for transfers between devices  359 us (67%)
  matrix products  66.3 us (12%)
  local copies, waits for them, and re-layouts  53.5 us (10%)
  starting transfers between devices  21.6 us (4%)
  other arithmetic  17.1 us (3%)
  between operations  14.5 us (3%)
    unnamed x6, waiting for transfers between devices  196 us
    ppermute x7, waiting for transfers between devices, search_rails_for(): obj = lax.ppermute(obj, axis_id, oldest)  164 us
    unnamed x33, local copies, waits for them, and re-layouts  26.2 us
    dot_general x5, matrix products, shards(): lax.dot_general(pad_up[tap_index:tap_index + row_count], dec_full[:, tap_...  18.1 us
    dot_general x5, matrix products, dec_terms(): jnp.dot(cot_full.T, pad_up[tap_index:tap_index + row_count], preferred_el...  12.8 us
    ppermute x4, starting transfers between devices, with_halo(): before = lax.ppermute(last, axis, up)  12.3 us
    dot_general x5, matrix products, shards(): jnp.dot(pad_cot[4 - tap_index:4 - tap_index + row_count], dec_full[:, tap...  11.6 us
    dynamic_update_slice x7, local copies, waits for them, and re-layouts, search_rails_for(): lax.dynamic_update_slice_in_dim(y2, obj, (z - tick) % w_next * outer, axi...  11 us
  transfers between devices with their start and end apart: 19, of which 8 were waited for; matrix products, arithmetic and copies ran while one was open for 21% of the time, Pallas kernels for 0%

profile of v1, /device:TPU:0, one launch (start us, length us, event | category | flops | bytes accessed | tf_op | source)
XLA Modules:
  0.0 534.9 jit_solution(13241130299326977567)
XLA Ops:
  7.9 3.0 collective-permute-start.3
  11.0 24.3 %collective-permute-done.3 = bf16[96,5,768]{2,0,1:T(8,128)(2,1)S(1)} collective-permute-done((bf16[96,5,768]{2,0,1:T(8,128)(2,1)}, bf16[96,5,768]{2,0,1:T(8,128)(2,1)S(1)}, u32[]{:S(2)}, u32[]{:S(2)}) %collective-permute-start.3) | collective-permute-done | bytes 737312 | tf_op jit(solution)/shard_map/ppermute | solution.py:18
  35.7 34.6 %collective-permute-done.4 = bf16[96,5,768]{2,0,1:T(8,128)(2,1)S(1)} collective-permute-done((bf16[96,5,768]{2,0,1:T(8,128)(2,1)S(1)}, bf16[96,5,768]{2,0,1:T(8,128)(2,1)S(1)}, u32[]{:S(2)}, u32[]{:S(2)}) %collective-permute-start.4) | collective-permute-done | bytes 737312 | tf_op jit(solution)/shard_map/ppermute | solution.py:18
  70.3 35.6 %collective-permute-done.5 = bf16[96,5,768]{2,0,1:T(8,128)(2,1)S(1)} collective-permute-done((bf16[96,5,768]{2,0,1:T(8,128)(2,1)S(1)}, bf16[96,5,768]{2,0,1:T(8,128)(2,1)S(1)}, u32[]{:S(2)}, u32[]{:S(2)}) %collective-permute-start.5) | collective-permute-done | bytes 737312 | tf_op jit(solution)/shard_map/ppermute | solution.py:18
  105.9 36.1 %collective-permute-done.6 = bf16[96,5,768]{2,0,1:T(8,128)(2,1)} collective-permute-done((bf16[96,5,768]{2,0,1:T(8,128)(2,1)S(1)}, bf16[96,5,768]{2,0,1:T(8,128)(2,1)}, u32[]{:S(2)}, u32[]{:S(2)}) %collective-permute-start.6) | collective-permute-done | bytes 737312 | tf_op jit(solution)/shard_map/ppermute | solution.py:18
  142.0 2.6 all_gather.7
  147.8 2.2 reshape.31
  149.9 1.9 reduce_sum.18
  151.8 17.2 %collective-permute-done.7 = bf16[96,5,768]{2,0,1:T(8,128)(2,1)} collective-permute-done((bf16[96,5,768]{2,0,1:T(8,128)(2,1)}, bf16[96,5,768]{2,0,1:T(8,128)(2,1)}, u32[]{:S(2)}, u32[]{:S(2)}) %collective-permute-start.7) | collective-permute-done | bytes 737312 | tf_op jit(solution)/shard_map/ppermute | solution.py:18
  171.0 4.5 collective-permute-start
  175.6 2.9 broadcast_in_dim.16
  179.6 7.7 %collective-permute-done.8 = bf16[96,5,768]{2,0,1:T(8,128)(2,1)} collective-permute-done((bf16[96,5,768]{2,0,1:T(8,128)(2,1)}, bf16[96,5,768]{2,0,1:T(8,128)(2,1)}, u32[]{:S(2)}, u32[]{:S(2)}) %collective-permute-start.8) | collective-permute-done | bytes 737312 | tf_op jit(solution)/shard_map/ppermute | solution.py:18
  189.2 2.1 constant_dynamic-update-slice_fusion.6
  191.2 2.1 constant_dynamic-update-slice_fusion.5
  193.3 2.1 constant_dynamic-update-slice_fusion.4
  195.3 2.1 constant_dynamic-update-slice_fusion.3
  197.4 8.2 %collective-permute-done.9 = bf16[96,5,768]{2,0,1:T(8,128)(2,1)S(1)} collective-permute-done((bf16[96,5,768]{2,0,1:T(8,128)(2,1)}, bf16[96,5,768]{2,0,1:T(8,128)(2,1)S(1)}, u32[]{:S(2)}, u32[]{:S(2)}) %collective-permute-start.9) | collective-permute-done | bytes 737312 | tf_op jit(solution)/shard_map/ppermute | solution.py:18
  206.5 2.1 fusion.40
  208.6 2.1 fusion.37
  210.6 2.1 fusion.33
  212.7 2.1 fusion.35
  214.8 3.4 fusion.1
  218.2 2.2 reshape.29
  220.4 1.9 reduce_sum.19
  229.4 2.2 fusion.50
  233.5 4.5 collective-permute-start.2
  238.8 3.5 fusion.38
  242.9 1.9 collective-permute-start.14
  247.9 2.7 fusion.29
  252.9 2.5 copy-done
  257.1 3.5 fusion.39
  260.6 3.5 fusion.36
  265.0 3.5 fusion.34
  269.3 4.1 add_convert_fusion
  273.4 1.9 fusion.3
  275.3 1.8 fusion.31
  277.1 1.8 fusion.27
  278.9 1.8 fusion.23
  280.7 2.6 fusion.26
  283.5 3.1 fusion.5
  287.8 3.0 fusion.7
  290.9 3.0 fusion.9
  293.9 1.8 fusion.11
  295.7 10.4 %pad_maximum_fusion = bf16[768,5,1536]{0,2,1:T(8,128)(2,1)} fusion(bf16[768,5,768]{0,2,1:T(8,128)(2,1)} %fusion.11, bf16[768,5,768]{0,2,1:T(8,128)(2,1)} %copy-done), kind=kLoop, calls=%fused_computation | loop fusion | flops 23592960 | bytes 23592960 | tf_op jit(solution)/shard_map/concatenate | solution.py:123
  306.1 15.1 %copy.16 = bf16[768,7680]{1,0:T(8,128)(2,1)} copy(bf16[768,7680]{0,1:T(8,128)(2,1)} %bitcast.125) | data formatting | bytes 23592960
  326.0 195.1 %reduce-scatter.9.cloned.1.call-done = bf16[96,7680]{1,0:T(8,128)(2,1)} async-done(((bf16[768,7680]{1,0:T(8,128)(2,1)}), bf16[96,7680]{1,0:T(8,128)(2,1)}) %reduce-scatter.9.cloned.1.call-update) | async-done | bytes 1474576
  521.1 2.7 copy.17
  525.0 2.2 copy.10
  (94 shorter events, 37.8 us)
Async XLA Ops:
  7.2 215.1 %all-gather.2.cloned.1.call-start = ((), (), s32[]{:S(2)}) async-start(), calls=%async_computation.2 | async-start | bytes 6635520 | tf_op jit(solution)/shard_map/all_gather | solution.py:52
  7.9 313.3 %all-reduce.2.cloned.1.call-start = ((), (), s32[]{:S(2)}) async-start(), calls=%async_computation.3 | async-start | bytes 786432 | tf_op jit(solution)/shard_map/psum | solution.py:103
  7.9 27.3 %collective-permute-start.3 = (bf16[96,5,768]{2,0,1:T(8,128)(2,1)}, bf16[96,5,768]{2,0,1:T(8,128)(2,1)S(1)}, u32[]{:S(2)}, u32[]{:S(2)}) collective-permute-start(bf16[96,5,768]{2,0,1:T(8,128)(2,1)} %param.6), channel_id=1, source_target_pairs={{0,2},{2,4},{4,6},{6,8},{8,10},{10,12},{12,14},{14,0},{1,3},{3,5},... | collective-permute-start | bytes 2211848 | tf_op jit(solution)/shard_map/ppermute | solution.py:18
  35.2 106.8 %copy-start.8 = (bf16[96,5,768]{2,0,1:T(8,128)(2,1)}, bf16[96,5,768]{2,0,1:T(8,128)(2,1)S(1)}, u32[]{:S(2)}) copy-start(bf16[96,5,768]{2,0,1:T(8,128)(2,1)S(1)} %collective-permute-done.3) | copy-start | bytes 2211844
  35.2 35.1 %collective-permute-start.4 = (bf16[96,5,768]{2,0,1:T(8,128)(2,1)S(1)}, bf16[96,5,768]{2,0,1:T(8,128)(2,1)S(1)}, u32[]{:S(2)}, u32[]{:S(2)}) collective-permute-start(bf16[96,5,768]{2,0,1:T(8,128)(2,1)S(1)} %collective-permute-done.3), channel_id=1, source_target_pairs={{0,2},{2,4},{4,6},{6,8},{8,10},{10,12},{12,14},{14,0},{1,3},{3,5},... | collective-permute-start | bytes 2211848 | tf_op jit(solution)/shard_map/ppermute | solution.py:18
  70.3 71.7 %copy-start.10 = (bf16[96,5,768]{2,0,1:T(8,128)(2,1)}, bf16[96,5,768]{2,0,1:T(8,128)(2,1)S(1)}, u32[]{:S(2)}) copy-start(bf16[96,5,768]{2,0,1:T(8,128)(2,1)S(1)} %collective-permute-done.4) | copy-start | bytes 2211844
  70.3 35.6 %collective-permute-start.5 = (bf16[96,5,768]{2,0,1:T(8,128)(2,1)S(1)}, bf16[96,5,768]{2,0,1:T(8,128)(2,1)S(1)}, u32[]{:S(2)}, u32[]{:S(2)}) collective-permute-start(bf16[96,5,768]{2,0,1:T(8,128)(2,1)S(1)} %collective-permute-done.4), channel_id=1, source_target_pairs={{0,2},{2,4},{4,6},{6,8},{8,10},{10,12},{12,14},{14,0},{1,3},{3,5},... | collective-permute-start | bytes 2211848 | tf_op jit(solution)/shard_map/ppermute | solution.py:18
  105.9 36.1 %copy-start.12 = (bf16[96,5,768]{2,0,1:T(8,128)(2,1)}, bf16[96,5,768]{2,0,1:T(8,128)(2,1)S(1)}, u32[]{:S(2)}) copy-start(bf16[96,5,768]{2,0,1:T(8,128)(2,1)S(1)} %collective-permute-done.5) | copy-start | bytes 2211844
  105.9 36.1 %collective-permute-start.6 = (bf16[96,5,768]{2,0,1:T(8,128)(2,1)S(1)}, bf16[96,5,768]{2,0,1:T(8,128)(2,1)}, u32[]{:S(2)}, u32[]{:S(2)}) collective-permute-start(bf16[96,5,768]{2,0,1:T(8,128)(2,1)S(1)} %collective-permute-done.5), channel_id=1, source_target_pairs={{0,2},{2,4},{4,6},{6,8},{8,10},{10,12},{12,14},{14,0},{1,3},{3,5},... | collective-permute-start | bytes 2211848 | tf_op jit(solution)/shard_map/ppermute | solution.py:18
  142.0 27.0 %collective-permute-start.7 = (bf16[96,5,768]{2,0,1:T(8,128)(2,1)}, bf16[96,5,768]{2,0,1:T(8,128)(2,1)}, u32[]{:S(2)}, u32[]{:S(2)}) collective-permute-start(bf16[96,5,768]{2,0,1:T(8,128)(2,1)} %collective-permute-done.6), channel_id=1, source_target_pairs={{0,2},{2,4},{4,6},{6,8},{8,10},{10,12},{12,14},{14,0},{1,3},{3,5},... | collective-permute-start | bytes 2211848 | tf_op jit(solution)/shard_map/ppermute | solution.py:18
  145.2 61.3 %collective-permute-start.12 = (bf16[2,768]{1,0:T(2,128)(2,1)}, bf16[2,768]{1,0:T(2,128)(2,1)S(1)}, u32[]{:S(2)}, u32[]{:S(2)}) collective-permute-start(bf16[2,768]{1,0:T(2,128)(2,1)} %get-tuple-element.17), channel_id=1, source_target_pairs={{0,2},{2,4},{4,6},{6,8},{8,10},{10,12},{12,14},{1,3},{3,5},{5,7},{... | collective-permute-start | bytes 9224 | tf_op jit(solution)/shard_map/ppermute | solution.py:34
  146.5 33.1 %collective-permute-start.11 = (bf16[2,768]{1,0:T(2,128)(2,1)}, bf16[2,768]{1,0:T(2,128)(2,1)S(1)}, u32[]{:S(2)}, u32[]{:S(2)}) collective-permute-start(bf16[2,768]{1,0:T(2,128)(2,1)} %get-tuple-element.16), channel_id=1, source_target_pairs={{2,0},{4,2},{6,4},{8,6},{10,8},{12,10},{14,12},{3,1},{5,3},{7,5},{... | collective-permute-start | bytes 9224 | tf_op jit(solution)/shard_map/ppermute | solution.py:35
  151.8 26.7 %copy-start.7 = (bf16[96,5,768]{2,0,1:T(8,128)(2,1)S(1)}, bf16[96,5,768]{2,0,1:T(8,128)(2,1)}, u32[]{:S(2)}) copy-start(bf16[96,5,768]{2,0,1:T(8,128)(2,1)} %param.6) | copy-start | bytes 2211844
  151.8 35.5 %copy-start.9 = (bf16[96,5,768]{2,0,1:T(8,128)(2,1)S(1)}, bf16[96,5,768]{2,0,1:T(8,128)(2,1)}, u32[]{:S(2)}) copy-start(bf16[96,5,768]{2,0,1:T(8,128)(2,1)} %copy-done.8) | copy-start | bytes 2211844
  169.0 18.3 %collective-permute-start.8 = (bf16[96,5,768]{2,0,1:T(8,128)(2,1)}, bf16[96,5,768]{2,0,1:T(8,128)(2,1)}, u32[]{:S(2)}, u32[]{:S(2)}) collective-permute-start(bf16[96,5,768]{2,0,1:T(8,128)(2,1)} %collective-permute-done.7), channel_id=1, source_target_pairs={{0,2},{2,4},{4,6},{6,8},{8,10},{10,12},{12,14},{14,0},{1,3},{3,5},... | collective-permute-start | bytes 2211848 | tf_op jit(solution)/shard_map/ppermute | solution.py:18
  169.1 19.2 %copy-start.11 = (bf16[96,5,768]{2,0,1:T(8,128)(2,1)S(1)}, bf16[96,5,768]{2,0,1:T(8,128)(2,1)}, u32[]{:S(2)}) copy-start(bf16[96,5,768]{2,0,1:T(8,128)(2,1)} %copy-done.10) | copy-start | bytes 2211844
  169.7 54.4 %collective-permute-start.1 = (bf16[2,768]{1,0:T(2,128)(2,1)}, bf16[2,768]{1,0:T(2,128)(2,1)}, u32[]{:S(2)}, u32[]{:S(2)}) collective-permute-start(bf16[2,768]{1,0:T(2,128)(2,1)} %get-tuple-element.25), channel_id=1, source_target_pairs={{2,0},{4,2},{6,4},{8,6},{10,8},{12,10},{14,12},{3,1},{5,3},{7,5},{... | collective-permute-start | bytes 9224 | tf_op jit(solution)/shard_map/ppermute | solution.py:35
  171.0 54.9 %collective-permute-start = (bf16[2,768]{1,0:T(2,128)(2,1)S(1)}, bf16[2,768]{1,0:T(2,128)(2,1)S(1)}, u32[]{:S(2)}, u32[]{:S(2)}) collective-permute-start(bf16[2,768]{1,0:T(2,128)(2,1)S(1)} %get-tuple-element.24), channel_id=1, source_target_pairs={{0,2},{2,4},{4,6},{6,8},{8,10},{10,12},{12,14},{1,3},{3,5},{5,7},{... | collective-permute-start | bytes 9224 | tf_op jit(solution)/shard_map/ppermute | solution.py:34
  187.3 18.3 %collective-permute-start.9 = (bf16[96,5,768]{2,0,1:T(8,128)(2,1)}, bf16[96,5,768]{2,0,1:T(8,128)(2,1)S(1)}, u32[]{:S(2)}, u32[]{:S(2)}) collective-permute-start(bf16[96,5,768]{2,0,1:T(8,128)(2,1)} %collective-permute-done.8), channel_id=1, source_target_pairs={{0,2},{2,4},{4,6},{6,8},{8,10},{10,12},{12,14},{14,0},{1,3},{3,5},... | collective-permute-start | bytes 2211848 | tf_op jit(solution)/shard_map/ppermute | solution.py:18
  232.2 23.2 %collective-permute-start.10 = (bf16[1,768]{1,0:T(2,128)(2,1)}, bf16[1,768]{1,0:T(2,128)(2,1)S(1)}, u32[]{:S(2)}, u32[]{:S(2)}) collective-permute-start(bf16[1,768]{1,0:T(2,128)(2,1)} %get-tuple-element.23), channel_id=1, source_target_pairs={{2,0},{4,2},{6,4},{8,6},{10,8},{12,10},{14,12},{3,1},{5,3},{7,5},{... | collective-permute-start | bytes 4616 | tf_op jit(solution)/shard_map/ppermute | solution.py:35
  233.5 21.9 %collective-permute-start.2 = (bf16[1,768]{1,0:T(2,128)(2,1)}, bf16[1,768]{1,0:T(2,128)(2,1)S(1)}, u32[]{:S(2)}, u32[]{:S(2)}) collective-permute-start(bf16[1,768]{1,0:T(2,128)(2,1)} %get-tuple-element.22), channel_id=1, source_target_pairs={{0,2},{2,4},{4,6},{6,8},{8,10},{10,12},{12,14},{1,3},{3,5},{5,7},{... | collective-permute-start | bytes 4616 | tf_op jit(solution)/shard_map/ppermute | solution.py:34
  238.8 11.8 %copy-start.4 = (bf16[512,768]{1,0:T(8,128)(2,1)}, bf16[512,768]{1,0:T(8,128)(2,1)S(1)}, u32[]{:S(2)}) copy-start(bf16[512,768]{1,0:T(8,128)(2,1)S(1)} %slice.174) | copy-start | bytes 2359300
  242.9 32.4 %collective-permute-start.14 = (bf16[2,768]{1,0:T(2,128)(2,1)}, bf16[2,768]{1,0:T(2,128)(2,1)S(1)}, u32[]{:S(2)}, u32[]{:S(2)}) collective-permute-start(bf16[2,768]{1,0:T(2,128)(2,1)} %get-tuple-element.19), channel_id=1, source_target_pairs={{0,2},{2,4},{4,6},{6,8},{8,10},{10,12},{12,14},{1,3},{3,5},{5,7},{... | collective-permute-start | bytes 9224 | tf_op jit(solution)/shard_map/ppermute | solution.py:34
  244.8 32.3 %collective-permute-start.13 = (bf16[2,768]{1,0:T(2,128)(2,1)}, bf16[2,768]{1,0:T(2,128)(2,1)}, u32[]{:S(2)}, u32[]{:S(2)}) collective-permute-start(bf16[2,768]{1,0:T(2,128)(2,1)} %get-tuple-element.18), channel_id=1, source_target_pairs={{2,0},{4,2},{6,4},{8,6},{10,8},{12,10},{14,12},{3,1},{5,3},{7,5},{... | collective-permute-start | bytes 9224 | tf_op jit(solution)/shard_map/ppermute | solution.py:35
  252.9 2.5 copy-start
  265.0 3.5 copy-start.5
  269.3 4.1 copy-start.6
  273.4 5.5 %copy-start.1 = (f32[256,768]{1,0:T(8,128)S(1)}, f32[256,768]{1,0:T(8,128)}, u32[]{:S(2)}) copy-start(f32[256,768]{1,0:T(8,128)} %fusion.29) | copy-start | bytes 2359300
  283.2 40.7 %reduce-scatter.7.cloned.1.call-start = ((), (), s32[]{:S(2)}) async-start(), calls=%async_computation.4 | async-start | bytes 1179648
  290.8 230.3 %reduce-scatter.9.cloned.1.call-start = ((), (), s32[]{:S(2)}) async-start(), calls=%async_computation.5 | async-start | bytes 13271040
  321.2 1.9 copy-start.3
  321.2 4.0 copy-start.2
Sparse Core Ops, SparseCore 0:
  10.2 142.0 all-gather.1
  283.4 22.0 all-reduce.1
  307.8 9.4 reduce-scatter.6
  321.3 199.7 reduce-scatter.8
